TPU v7x, 32 devices: a whole 2x2x4 slice. The times are simulated.
32 devices in a mesh: dp: 8 (over z, core), ctx: 4 (over y, x).
Axes of the slice: x: 2, y: 2, z: 4, core: 2. Of those that a mesh axis runs over, the one named last changes fastest.
Arguments:
- video: bfloat16 [64, 32, 64, 128], P('dp', 'ctx'), parts along dimension 0, may hold values from -6 to 6
- conv_weight: bfloat16 [3, 3, 3, 128, 256], replicated, may hold values from -0.109375 to 0.109375
- latent_weight: bfloat16 [256, 16], replicated, may hold values from -0.375 to 0.375
- embed_weight: bfloat16 [64, 3072], replicated, may hold values from -0.75 to 0.75
- modulation: float32 [32, 3072], P('dp'), parts along dimension 0, may hold values from -3 to 3
- qkv_weight: bfloat16 [3072, 3, 2048], P(None, None, 'ctx'), may hold values from -0.109375 to 0.109375
- qk_gain: float32 [2, 128], replicated, may hold values from 0.5 to 2
- text: bfloat16 [2048, 3072], P('dp'), parts along dimension 0, may hold values from -6 to 6
- text_weight: bfloat16 [3072, 2, 2048], P(None, None, 'ctx'), may hold values from -0.109375 to 0.109375
Outputs:
- attended: bfloat16 [8192, 2048], P(('dp', 'ctx')), parts along dimension 0
There are 8 independent parts, one for each index of `dp`. A program takes and returns all parts, laid end to end along the dimension named above; an argument that names none is the same for every part. Nothing has to cross between parts.
All inputs are finite; a program needn't handle non-finite values.
Results may differ from a plain program's by a relative error of at most 0.0074.
Values may be sent and summed in bfloat16 or wider, within the bound.
No kernel may reach another device: no remote copies, remote signals or barrier semaphores. Data moves between devices by JAX's collectives and lax.ppermute only.
A program may use at most 128 MiB of HBM per device.

v0:
```python
import math
import jax
import jax.numpy as jnp
from jax import lax
from jax.sharding import PartitionSpec as P

D = 3072
HS = 128


def shifted(x, axis, by):
    devices = lax.axis_size(axis)
    pairs = [(i, i + by) for i in range(devices) if 0 <= i + by < devices]
    return lax.ppermute(x, axis, pairs)


def layer_norm(values):
    centred = values - jnp.mean(values, -1, keepdims=True)
    return centred * lax.rsqrt(jnp.mean(centred * centred, -1, keepdims=True) + 1e-06)


def head_norm(values, gain):
    return values * lax.rsqrt(jnp.mean(values * values, -1, keepdims=True) + 1e-06) * gain


def patchify(latent):
    frames, rows, cols, chans = latent.shape
    shaped = latent.reshape(frames, rows // 2, 2, cols // 2, 2, chans)
    return shaped.transpose(0, 1, 3, 2, 4, 5).reshape(frames, rows // 2, cols // 2, 4 * chans)


def attend(query_block, key_rows, value_rows):
    logits = jnp.einsum(
        "bhd,khd->hbk", query_block, key_rows, preferred_element_type=jnp.float32
    ) / math.sqrt(HS)
    expd = jnp.exp(logits - jnp.max(logits, -1, keepdims=True))
    weights = (expd / jnp.sum(expd, -1, keepdims=True)).astype(jnp.bfloat16)
    return jnp.einsum(
        "hbk,khd->bhd", weights, value_rows, preferred_element_type=jnp.float32
    ).astype(jnp.bfloat16)


def shards(
    video,
    conv_weight,
    latent_weight,
    embed_weight,
    modulation,
    qkv_weight,
    qk_gain,
    text,
    text_weight,
):
    upper_rim = shifted(video[:, -1:], "ctx", 1)
    framed = jnp.concatenate([upper_rim, video], 1)
    framed = jnp.concatenate([framed[:1], framed[:1], framed], 0)
    framed = jnp.pad(framed, ((0, 0), (0, 0), (1, 0), (0, 0)))
    conv = lax.conv_general_dilated(
        framed[None],
        conv_weight,
        (1, 2, 2),
        "VALID",
        dimension_numbers=("NDHWC", "DHWIO", "NDHWC"),
        preferred_element_type=jnp.float32,
    )[0]
    activated = jax.nn.silu(conv).astype(jnp.bfloat16)
    latent = jnp.dot(activated, latent_weight, preferred_element_type=jnp.float32).astype(
        jnp.bfloat16
    )
    tile_patches = patchify(latent)
    width_in = tile_patches.shape[3]
    token_rows = lax.all_to_all(
        tile_patches, "ctx", split_axis=0, concat_axis=1, tiled=True
    ).reshape(-1, width_in)
    embedded = jnp.dot(token_rows, embed_weight, preferred_element_type=jnp.float32)
    stream = (layer_norm(embedded) * (1.0 + modulation[1]) + modulation[0]).astype(jnp.bfloat16)
    text_stream = (
        layer_norm(text.astype(jnp.float32)) * (1.0 + modulation[3]) + modulation[2]
    ).astype(jnp.bfloat16)
    text_count = text.shape[0]
    local_heads = qkv_weight.shape[2] // HS
    flat_weight = qkv_weight.reshape(D, -1)
    projected = jnp.dot(
        lax.all_gather(stream, "ctx", axis=0, tiled=True),
        flat_weight,
        preferred_element_type=jnp.float32,
    )
    count = projected.shape[0]
    projected = projected.reshape(count, 3, local_heads, HS)
    queries = head_norm(projected[:, 0], qk_gain[0]).astype(jnp.bfloat16)
    keys_own = head_norm(projected[:, 1], qk_gain[1]).astype(jnp.bfloat16)
    values_own = projected[:, 2].astype(jnp.bfloat16)
    text_projected = jnp.dot(
        text_stream, text_weight.reshape(D, -1), preferred_element_type=jnp.float32
    )
    text_projected = text_projected.reshape(text_count, 2, local_heads, HS)
    text_keys = head_norm(text_projected[:, 0], qk_gain[1]).astype(jnp.bfloat16)
    text_values = text_projected[:, 1].astype(jnp.bfloat16)
    key_rows = jnp.concatenate([text_keys, keys_own], 0)
    value_rows = jnp.concatenate([text_values, values_own], 0)
    block = 512 if count % 512 == 0 else count
    blocks = queries.reshape(count // block, block, local_heads, HS)
    result = lax.map(lambda query_block: attend(query_block, key_rows, value_rows), blocks)
    result = result.reshape(count, local_heads * HS)
    return lax.all_to_all(result, "ctx", split_axis=0, concat_axis=1, tiled=True)


def solution(mesh):
    in_specs = (
        P("dp", "ctx", None, None),
        P(),
        P(),
        P(),
        P("dp", None),
        P(None, None, "ctx"),
        P(),
        P("dp", None),
        P(None, None, "ctx"),
    )
    out_specs = P(("dp", "ctx"), None)
    return jax.shard_map(shards, mesh=mesh, in_specs=in_specs, out_specs=out_specs, check_vma=False)
```

profile of v0, /device:TPU:0, one launch (start us, length us, event | category | flops | bytes accessed | tf_op | source)
XLA Modules:
  0.0 192.1 jit_solution(4728737379839621711)
XLA Ops:
  7.6 4.8 %collective-permute-start = (bf16[8,1,64,128]{3,2,1,0:T(8,128)(2,1)S(1)}, bf16[8,1,64,128]{3,2,1,0:T(8,128)(2,1)S(1)}, u32[]{:S(2)}, u32[]{:S(2)}) collective-permute-start(bf16[8,1,64,128]{3,2,1,0:T(8,128)(2,1)S(1)} %slice.43), channel_id=1, source_target_pairs={{0,1},{1,2},{2,3},{4,5},{5,6},{6,7},{8,9},{9,10},{10,11},{12,13},{... | collective-permute-start | bytes 393224 | tf_op jit(solution)/shard_map/ppermute | solution.py:14
  12.4 2.7 %collective-permute-done = bf16[8,1,64,128]{3,2,1,0:T(8,128)(2,1)S(1)} collective-permute-done((bf16[8,1,64,128]{3,2,1,0:T(8,128)(2,1)S(1)}, bf16[8,1,64,128]{3,2,1,0:T(8,128)(2,1)S(1)}, u32[]{:S(2)}, u32[]{:S(2)}) %collective-permute-start) | collective-permute-done | bytes 131104 | tf_op jit(solution)/shard_map/ppermute | solution.py:14
  18.7 4.6 %reshape.97 = bf16[10,9,1,8,10,128]{5,4,3,1,0,2:T(8,128)(2,1)} reshape(bf16[10,9,1,80,128]{4,3,1,0,2:T(8,128)(2,1)} %pad.5) | data formatting | bytes 3686400 | tf_op jit(solution)/shard_map/conv_general_dilated | solution.py:58
  23.3 2.4 %copy.26 = bf16[10,9,1,8,10,128]{5,3,4,1,0,2:T(8,128)(2,1)S(1)} copy(bf16[10,9,1,8,10,128]{5,4,3,1,0,2:T(8,128)(2,1)} %reshape.97) | data formatting | bytes 3686400 | tf_op jit(solution)/shard_map/conv_general_dilated | solution.py:58
  25.9 2.6 %fusion.57 = f32[8,4,8,5,256]{4,2,3,1,0:T(8,128)S(1)} fusion(bf16[3,3,3,128,256]{4,3,2,1,0:T(8,128)(2,1)S(1)} %copy-done, bf16[10,9,1,7,2,128]{5,3,4,1,0,2:T(8,128)(2,1)S(1)} %slice.59, bf16[10,9,1,8,10,128]{5,3,4,1,0,2:T(8,128)(2,1)S(1)} %copy.26, pred[8,5]{0,1:T(8,128)(4,1)S(1)} %copy-done.9), kind=kOutput, calls=%fused_computation.60 | convolution fusion | flops 2271887360 | bytes 5245992 | tf_op jit(solution)/shard_map/conv_general_dilated | solution.py:58
  31.5 4.7 %all-to-all-start = ((bf16[4,2,2048]{2,1,0:T(2,128)(2,1)}), bf16[4,2,2048]{2,1,0:T(2,128)(2,1)S(1)}, u32[]{:S(2)}, u32[]{:S(2)}) async-start(bf16[4,2,2048]{2,1,0:T(2,128)(2,1)} %reshape.112), calls=%async_computation | async-start | bytes 65536 | tf_op jit(solution)/shard_map/all_to_all | solution.py:72
  36.2 4.7 %all-to-all-done = bf16[4,2,2048]{2,1,0:T(2,128)(2,1)S(1)} async-done(((bf16[4,2,2048]{2,1,0:T(2,128)(2,1)}), bf16[4,2,2048]{2,1,0:T(2,128)(2,1)S(1)}, u32[]{:S(2)}, u32[]{:S(2)}) %all-to-all-start) | async-done | bytes 32800 | tf_op jit(solution)/shard_map/all_to_all | solution.py:72
  42.2 1.9 add_convert_fusion
  44.1 12.9 %copy.32 = bf16[3072,3,512]{0,2,1:T(8,128)(2,1)} copy(bf16[3072,3,512]{2,0,1:T(8,128)(2,1)} %param.16) | data formatting | bytes 18874368 | tf_op args[5]
  57.0 7.5 %copy.47 = bf16[384,8,2,512]{3,1,2,0:T(8,128)(2,1)} copy(bf16[384,8,2,512]{3,2,1,0:T(2,128)(2,1)} %bitcast.112) | data formatting | bytes 12582912
  64.5 8.8 %copy.35 = bf16[1024,3072]{1,0:T(8,128)(2,1)} copy(bf16[1024,3072]{0,1:T(8,128)(2,1)} %bitcast.109) | data formatting | bytes 12582912 | tf_op jit(solution)/shard_map/dot_general | solution.py:93
  74.2 4.0 %fusion.51 = f32[256,2,4,128]{3,0,2,1:T(8,128)S(1)} fusion(bf16[2,4,128,3072]{3,2,1,0:T(8,128)(2,1)} %bitcast.113, bf16[256,3072]{1,0:T(8,128)(2,1)S(1)} %copy-done.2, f32[3072]{0:T(1024)S(1)} %bitcast.124, f32[3072]{0:T(1024)S(1)} %bitcast.123, f32[256]{0:T(256)S(1)} %add_rsqrt_fusion.3, f32[256]{0:T(256)S(1)} %broadcast_multiply_fusion), kind=kOutput, calls=%fused_computation.55 | convolution fusion | flops 1615331328 | bytes 8939520 | tf_op jit(solution)/shard_map/dot_general | solution.py:93
  78.7 35.2 %all-gather.2.cloned.1.call-done = bf16[1024,3072]{1,0:T(8,128)(2,1)} async-done(((bf16[256,3072]{1,0:T(8,128)(2,1)}), bf16[1024,3072]{1,0:T(8,128)(2,1)}) %all-gather.2.cloned.1.call-update) | async-done | bytes 6291472 | tf_op jit(solution)/shard_map/all_gather | solution.py:84
  113.9 13.3 %fusion.26 = f32[1024,3,4,128]{3,0,2,1:T(8,128)S(1)} fusion(bf16[3,4,128,3072]{3,2,1,0:T(8,128)(2,1)} %bitcast.110, bf16[1024,3072]{1,0:T(8,128)(2,1)} %all-gather.2.cloned.1.call-done), kind=kOutput, calls=%fused_computation.19 | convolution fusion | flops 9663676416 | bytes 22020096 | tf_op jit(solution)/shard_map/dot_general | solution.py:83
  129.3 1.5 fusion.46
  132.1 31.1 %while.10 = (s32[]{:T(128)}, bf16[2,512,4,128]{3,2,1,0:T(4,128)(2,1)}, bf16[2,512,4,128]{3,1,2,0:T(8,128)(2,1)}, bf16[1280,4,128]{2,0,1:T(8,128)(2,1)S(1)}, bf16[1280,4,128]{2,0,1:T(8,128)(2,1)}, /*index=5*/s32[]{:T(128)}) while((s32[]{:T(128)}, bf16[2,512,4,128]{3,2,1,0:T(4,128)(2,1)}, bf16[2,512,4,128]{3,1,2,0:T(8,128)(2,1)}, ...), condition=%wide.region_10.11_spmd, body=%wide.region_7.10_spmd.sunk | while | flops 1355547904 | bytes 34095744 | solution.py:103
  132.1 8.1 %fusion.90 = (f32[4,512]{1,0:T(4,128)S(1)}, f32[4,512,1280]{2,1,0:T(8,128)}) fusion(bf16[1280,4,128]{2,0,1:T(8,128)(2,1)S(1)} %get-tuple-element.107, bf16[2,512,4,128]{3,1,2,0:T(8,128)(2,1)} %get-tuple-element.106, s32[]{:T(128)} %get-tuple-element.98), kind=kOutput, calls=%fused_computation.91.clone.1 | convolution fusion | flops 678954240 | bytes 12329472 | tf_op jit(solution)/shard_map/while/body/eval_jaxpr/sub | solution.py:36
  140.3 6.0 %fusion.91 = bf16[1,512,4,128]{3,1,2,0:T(8,128)(2,1)S(1)} fusion(bf16[1280,4,128]{2,0,1:T(8,128)(2,1)} %get-tuple-element.108, f32[4,512,1280]{2,1,0:T(8,128)} %get-tuple-element.90, f32[4,512]{1,0:T(4,128)S(1)} %get-tuple-element.91), kind=kOutput, calls=%fused_computation.8.clone.1 | convolution fusion | flops 676593664 | bytes 12328960 | tf_op jit(solution)/shard_map/while/body/eval_jaxpr/hbk,khd->bhd/dot_general | solution.py:38
  147.7 8.1 %fusion.90 = (f32[4,512]{1,0:T(4,128)S(1)}, f32[4,512,1280]{2,1,0:T(8,128)}) fusion(bf16[1280,4,128]{2,0,1:T(8,128)(2,1)S(1)} %get-tuple-element.107, bf16[2,512,4,128]{3,1,2,0:T(8,128)(2,1)} %get-tuple-element.106, s32[]{:T(128)} %get-tuple-element.98), kind=kOutput, calls=%fused_computation.91.clone.1 | convolution fusion | flops 678954240 | bytes 12329472 | tf_op jit(solution)/shard_map/while/body/eval_jaxpr/sub | solution.py:36
  155.8 6.0 %fusion.91 = bf16[1,512,4,128]{3,1,2,0:T(8,128)(2,1)S(1)} fusion(bf16[1280,4,128]{2,0,1:T(8,128)(2,1)} %get-tuple-element.108, f32[4,512,1280]{2,1,0:T(8,128)} %get-tuple-element.90, f32[4,512]{1,0:T(4,128)S(1)} %get-tuple-element.91), kind=kOutput, calls=%fused_computation.8.clone.1 | convolution fusion | flops 676593664 | bytes 12328960 | tf_op jit(solution)/shard_map/while/body/eval_jaxpr/hbk,khd->bhd/dot_general | solution.py:38
  163.2 1.5 all_to_all.28
  164.7 17.7 %all_to_all.34 = bf16[4,256,512]{2,1,0:T(8,128)(2,1)} all-to-all(bf16[4,256,512]{2,1,0:T(8,128)(2,1)S(1)} %all_to_all.28), channel_id=1, replica_groups=mesh['dp'=8,'ctx'=4] {'ctx'}, dimensions={0} | all-to-all | bytes 2097152 | tf_op jit(solution)/shard_map/all_to_all | solution.py:105
  182.4 1.5 copy.37
  183.9 1.4 copy.38
  (66 shorter events, 16.4 us)
Async XLA Ops:
  6.5 19.3 %copy-start = (bf16[3,3,3,128,256]{4,3,2,1,0:T(8,128)(2,1)S(1)}, bf16[3,3,3,128,256]{4,3,2,1,0:T(8,128)(2,1)}, u32[]{:S(2)}) copy-start(bf16[3,3,3,128,256]{4,3,2,1,0:T(8,128)(2,1)} %param.12) | copy-start | bytes 5308420
  7.6 7.6 %collective-permute-start = (bf16[8,1,64,128]{3,2,1,0:T(8,128)(2,1)S(1)}, bf16[8,1,64,128]{3,2,1,0:T(8,128)(2,1)S(1)}, u32[]{:S(2)}, u32[]{:S(2)}) collective-permute-start(bf16[8,1,64,128]{3,2,1,0:T(8,128)(2,1)S(1)} %slice.43), channel_id=1, source_target_pairs={{0,1},{1,2},{2,3},{4,5},{5,6},{6,7},{8,9},{9,10},{10,11},{12,13},{... | collective-permute-start | bytes 393224 | tf_op jit(solution)/shard_map/ppermute | solution.py:14
  23.3 2.6 %copy-start.9 = (pred[8,5]{0,1:T(8,128)(4,1)S(1)}, pred[8,5]{0,1:T(8,128)(4,1)}, u32[]{:S(2)}) copy-start(pred[8,5]{0,1:T(8,128)(4,1)} %constant.50) | copy-start | bytes 124
  28.5 1.1 copy-start.8
  28.5 7.7 %copy-start.6 = (f32[4,3072]{1,0:T(4,128)S(1)}, f32[4,3072]{1,0:T(4,128)}, u32[]{:S(2)}) copy-start(f32[4,3072]{1,0:T(4,128)} %param.15) | copy-start | bytes 147460
  29.3 11.8 %copy-start.5 = (bf16[64,3072]{1,0:T(8,128)(2,1)S(1)}, bf16[64,3072]{1,0:T(8,128)(2,1)}, u32[]{:S(2)}) copy-start(bf16[64,3072]{1,0:T(8,128)(2,1)} %param.14) | copy-start | bytes 1179652
  31.5 9.5 %all-to-all-start = ((bf16[4,2,2048]{2,1,0:T(2,128)(2,1)}), bf16[4,2,2048]{2,1,0:T(2,128)(2,1)S(1)}, u32[]{:S(2)}, u32[]{:S(2)}) async-start(bf16[4,2,2048]{2,1,0:T(2,128)(2,1)} %reshape.112), calls=%async_computation | async-start | bytes 65536 | tf_op jit(solution)/shard_map/all_to_all | solution.py:72
  36.2 77.7 %all-gather.2.cloned.1.call-start = ((), (), s32[]{:S(2)}) async-start(), calls=%async_computation.2 | async-start | bytes 7864320 | tf_op jit(solution)/shard_map/all_gather | solution.py:84
  64.5 8.8 %copy-start.2 = (bf16[256,3072]{1,0:T(8,128)(2,1)S(1)}, bf16[256,3072]{1,0:T(8,128)(2,1)}, u32[]{:S(2)}) copy-start(bf16[256,3072]{1,0:T(8,128)(2,1)} %param.18) | copy-start | bytes 4718596
  74.2 4.2 %copy-start.7 = (f32[2,128]{1,0:T(2,128)S(1)}, f32[2,128]{1,0:T(2,128)}, u32[]{:S(2)}) copy-start(f32[2,128]{1,0:T(2,128)} %param.17) | copy-start | bytes 3076
  140.3 6.0 %copy-start.3 = (bf16[2,512,4,128]{3,2,1,0:T(4,128)(2,1)S(1)}, bf16[2,512,4,128]{3,2,1,0:T(4,128)(2,1)}, u32[]{:S(2)}) copy-start(bf16[2,512,4,128]{3,2,1,0:T(4,128)(2,1)} %get-tuple-element.99) | copy-start | bytes 3145732 | tf_op jit(solution)/shard_map/while
  146.7 1.0 copy-start.4
  155.8 6.0 %copy-start.3 = (bf16[2,512,4,128]{3,2,1,0:T(4,128)(2,1)S(1)}, bf16[2,512,4,128]{3,2,1,0:T(4,128)(2,1)}, u32[]{:S(2)}) copy-start(bf16[2,512,4,128]{3,2,1,0:T(4,128)(2,1)} %get-tuple-element.99) | copy-start | bytes 3145732 | tf_op jit(solution)/shard_map/while
  162.2 1.0 copy-start.4
  164.7 20.6 %copy-start.1 = (bf16[3,3,3,128,256]{4,3,2,1,0:T(8,128)(2,1)S(1)}, bf16[3,3,3,128,256]{4,3,2,1,0:T(8,128)(2,1)}, u32[]{:S(2)}) copy-start(bf16[3,3,3,128,256]{4,3,2,1,0:T(8,128)(2,1)} %param.12) | copy-start | bytes 5308420
Sparse Core Ops, SparseCore 0:
  44.2 69.6 all-gather.1
where the time goes:
time: 193 us; the launch traced here: 192 us
  local copies, waits for them, and re-layouts  49.8 us (26%)
  matrix products  49.2 us (25%)
  waiting for transfers between devices  42.6 us (22%)
  blocking collectives  17.7 us (9%)
  between operations  13.7 us (7%)
  starting transfers between devices  9.56 us (5%)
  other arithmetic  9.49 us (5%)
    all_gather x1, waiting for transfers between devices, shards(): lax.all_gather(stream, 'ctx', axis=0, tiled=True)  35.2 us
    unnamed x21, local copies, waits for them, and re-layouts  21.3 us
    all_to_all x1, blocking collectives, shards(): lax.all_to_all(result, 'ctx', split_axis=0, concat_axis=1, tiled=True)  17.7 us
    sub x2, matrix products, attend(): expd = jnp.exp(logits - jnp.max(logits, -1, keepdims=True))  16.3 us
    dot_general x1, matrix products, shards(): jnp.dot(lax.all_gather(stream, 'ctx', axis=0, tiled=True), flat_weight, p...  13.3 us
    dot_general x2, matrix products, attend(): jnp.einsum('hbk,khd->bhd', weights, value_rows, preferred_element_type=jn...  11.9 us
    dot_general x1, local copies, waits for them, and re-layouts, shards(): jnp.dot(text_stream, text_weight.reshape(D, -1), preferred_element_type=j...  8.79 us
    conv_general_dilated x4, local copies, waits for them, and re-layouts, shards(): lax.conv_general_dilated(framed[None], conv_weight, (1, 2, 2), 'VALID', d...  7.91 us
  transfers between devices with their start and end apart: 3, of which 3 were waited for; matrix products, arithmetic and copies ran while one was open for 18% of the time, Pallas kernels for 0%

commit v1 on v0

--- a/solution.py
+++ b/solution.py
@@ -6,6 +6,28 @@
 
 D = 3072
 HS = 128
+
+
+def joined_along(pieces, dim):
+    lengths = list(pieces.shape[1:])
+    lengths[dim] *= pieces.shape[0]
+    return jnp.moveaxis(pieces, 0, dim).reshape(lengths)
+
+
+def doubled(x, axis):
+    length = lax.axis_size(axis)
+    parts = x[None]
+    for level in range(length.bit_length() - 1):
+        bit = 1 << level
+        theirs = lax.ppermute(parts, axis, [(i, i ^ bit) for i in range(length)])
+        both = jnp.stack([parts, theirs])
+        upper = lax.axis_index(axis) >> level & 1
+        parts = jnp.where(upper == 0, both, both[::-1]).reshape(-1, *x.shape)
+    return parts
+
+
+def gather_by_bits(array, axis, dim):
+    return joined_along(doubled(array, axis), dim)
 
 
 def shifted(x, axis, by):
@@ -81,9 +103,7 @@
     local_heads = qkv_weight.shape[2] // HS
     flat_weight = qkv_weight.reshape(D, -1)
     projected = jnp.dot(
-        lax.all_gather(stream, "ctx", axis=0, tiled=True),
-        flat_weight,
-        preferred_element_type=jnp.float32,
+        gather_by_bits(stream, "ctx", 0), flat_weight, preferred_element_type=jnp.float32
     )
     count = projected.shape[0]
     projected = projected.reshape(count, 3, local_heads, HS)

time: 193 us -> 215 us (1.11)
  waiting for transfers between devices: 42.6 us -> 67.9 us
  other arithmetic: 9.49 us -> 24.6 us
  between operations: 13.7 us -> 0.38 us
  blocking collectives: 17.7 us -> 13.6 us
    ppermute x0 -> x2, waiting for transfers between devices: none -> 61.1 us  [doubled(): theirs = lax.ppermute(parts, axis, [(i, i ^ bit) for i in range(length)])]
    all_gather x1 -> x0, waiting for transfers between devices: 35.2 us -> none  [shards(): lax.all_gather(stream, 'ctx', axis=0, tiled=True)]
    another operation x0 -> x4, other arithmetic: none -> 7.69 us  [doubled(): both = jnp.stack([parts, theirs])]
    select_n x0 -> x1, other arithmetic: none -> 4.36 us  [doubled(): parts = jnp.where(upper == 0, both, both[::-1]).reshape(-1, *x.shape)]
    all_to_all x1, blocking collectives: 17.7 us -> 13.6 us  [shards(): lax.all_to_all(result, 'ctx', split_axis=0, concat_axis=1, tiled=True)]
    unnamed x21 -> x37, local copies, waits for them, and re-layouts: 21.3 us -> 21.1 us
  transfers between devices with their start and end apart: 3 -> 4, of which waited for: 3 -> 4; matrix products, arithmetic and copies ran while one was open for 18% -> 18% of each run, Pallas kernels for 0% -> 0%
where the time goes in v1:
time: 215 us; the launch traced here: 214 us
  waiting for transfers between devices  67.9 us (32%)
  local copies, waits for them, and re-layouts  49.2 us (23%)
  matrix products  47.4 us (22%)
  other arithmetic  24.6 us (11%)
  blocking collectives  13.6 us (6%)
  starting transfers between devices  11 us (5%)
    ppermute x2, waiting for transfers between devices, doubled(): theirs = lax.ppermute(parts, axis, [(i, i ^ bit) for i in range(length)])  61.1 us
    unnamed x37, local copies, waits for them, and re-layouts  21.1 us
    sub x2, matrix products, attend(): expd = jnp.exp(logits - jnp.max(logits, -1, keepdims=True))  16.3 us
    all_to_all x1, blocking collectives, shards(): lax.all_to_all(result, 'ctx', split_axis=0, concat_axis=1, tiled=True)  13.6 us
    dot_general x1, matrix products, shards(): jnp.dot(gather_by_bits(stream, 'ctx', 0), flat_weight, preferred_element_...  12.3 us
    dot_general x2, matrix products, attend(): jnp.einsum('hbk,khd->bhd', weights, value_rows, preferred_element_type=jn...  11.1 us
    dot_general x1, local copies, waits for them, and re-layouts, shards(): jnp.dot(text_stream, text_weight.reshape(D, -1), preferred_element_type=j...  8.7 us
    conv_general_dilated x4, local copies, waits for them, and re-layouts, shards(): lax.conv_general_dilated(framed[None], conv_weight, (1, 2, 2), 'VALID', d...  7.92 us
  transfers between devices with their start and end apart: 4, of which 4 were waited for; matrix products, arithmetic and copies ran while one was open for 18% of the time, Pallas kernels for 0%

profile of v1, /device:TPU:0, one launch (start us, length us, event | category | flops | bytes accessed | tf_op | source)
XLA Modules:
  0.0 214.1 jit_solution(9160654831365593848)
XLA Ops:
  1.1 4.8 %collective-permute-start = (bf16[8,1,64,128]{3,2,1,0:T(8,128)(2,1)S(1)}, bf16[8,1,64,128]{3,2,1,0:T(8,128)(2,1)S(1)}, u32[]{:S(2)}, u32[]{:S(2)}) collective-permute-start(bf16[8,1,64,128]{3,2,1,0:T(8,128)(2,1)S(1)} %slice.43), channel_id=1, source_target_pairs={{0,1},{1,2},{2,3},{4,5},{5,6},{6,7},{8,9},{9,10},{10,11},{12,13},{... | collective-permute-start | bytes 393224 | tf_op jit(solution)/shard_map/ppermute | solution.py:36
  5.9 2.7 %collective-permute-done = bf16[8,1,64,128]{3,2,1,0:T(8,128)(2,1)S(1)} collective-permute-done((bf16[8,1,64,128]{3,2,1,0:T(8,128)(2,1)S(1)}, bf16[8,1,64,128]{3,2,1,0:T(8,128)(2,1)S(1)}, u32[]{:S(2)}, u32[]{:S(2)}) %collective-permute-start) | collective-permute-done | bytes 131104 | tf_op jit(solution)/shard_map/ppermute | solution.py:36
  12.2 4.6 %reshape.101 = bf16[10,9,1,8,10,128]{5,4,3,1,0,2:T(8,128)(2,1)} reshape(bf16[10,9,1,80,128]{4,3,1,0,2:T(8,128)(2,1)} %pad.5) | data formatting | bytes 3686400 | tf_op jit(solution)/shard_map/conv_general_dilated | solution.py:80
  16.8 2.4 %copy.26 = bf16[10,9,1,8,10,128]{5,3,4,1,0,2:T(8,128)(2,1)S(1)} copy(bf16[10,9,1,8,10,128]{5,4,3,1,0,2:T(8,128)(2,1)} %reshape.101) | data formatting | bytes 3686400 | tf_op jit(solution)/shard_map/conv_general_dilated | solution.py:80
  19.4 2.6 %fusion.57 = f32[8,4,8,5,256]{4,2,3,1,0:T(8,128)S(1)} fusion(bf16[3,3,3,128,256]{4,3,2,1,0:T(8,128)(2,1)S(1)} %copy-done, bf16[10,9,1,7,2,128]{5,3,4,1,0,2:T(8,128)(2,1)S(1)} %slice.59, bf16[10,9,1,8,10,128]{5,3,4,1,0,2:T(8,128)(2,1)S(1)} %copy.26, pred[8,5]{0,1:T(8,128)(4,1)S(1)} %copy-done.12), kind=kOutput, calls=%fused_computation.64 | convolution fusion | flops 2271887360 | bytes 5245992 | tf_op jit(solution)/shard_map/conv_general_dilated | solution.py:80
  24.9 4.7 %all-to-all-start = ((bf16[4,2,2048]{2,1,0:T(2,128)(2,1)}), bf16[4,2,2048]{2,1,0:T(2,128)(2,1)S(1)}, u32[]{:S(2)}, u32[]{:S(2)}) async-start(bf16[4,2,2048]{2,1,0:T(2,128)(2,1)} %reshape.116), calls=%async_computation | async-start | bytes 65536 | tf_op jit(solution)/shard_map/all_to_all | solution.py:94
  30.3 4.1 %all-to-all-done = bf16[4,2,2048]{2,1,0:T(2,128)(2,1)S(1)} async-done(((bf16[4,2,2048]{2,1,0:T(2,128)(2,1)}), bf16[4,2,2048]{2,1,0:T(2,128)(2,1)S(1)}, u32[]{:S(2)}, u32[]{:S(2)}) %all-to-all-start) | async-done | bytes 32800 | tf_op jit(solution)/shard_map/all_to_all | solution.py:94
  38.9 32.7 %collective-permute-done.1 = bf16[1,256,3072]{2,1,0:T(8,128)(2,1)} collective-permute-done((bf16[1,256,3072]{2,1,0:T(8,128)(2,1)}, bf16[1,256,3072]{2,1,0:T(8,128)(2,1)}, u32[]{:S(2)}, u32[]{:S(2)}) %collective-permute-start.1) | collective-permute-done | bytes 1572896 | tf_op jit(solution)/shard_map/ppermute | solution.py:22
  73.4 2.7 %fusion.37 = (bf16[1,2,256,3072]{3,2,1,0:T(8,128)(2,1)S(1)}, bf16[2,256,3072]{2,1,0:T(8,128)(2,1)}) fusion(bf16[2,1,256,3072]{3,2,1,0:T(8,128)(2,1)S(1)} %pad_maximum_fusion.1, pred[]{:T(512)S(6)} %eq.7), kind=kLoop, calls=%fused_computation.40 | loop fusion | flops 1572864 | bytes 9437185 | tf_op jit(solution)/shard_map/stack;reshape | solution.py:23
  76.7 12.7 %copy.32 = bf16[3072,3,512]{0,2,1:T(8,128)(2,1)} copy(bf16[3072,3,512]{2,0,1:T(8,128)(2,1)} %param.16) | data formatting | bytes 18874368 | tf_op args[5]
  89.4 7.4 %copy.47 = bf16[384,8,2,512]{3,1,2,0:T(8,128)(2,1)} copy(bf16[384,8,2,512]{3,2,1,0:T(2,128)(2,1)} %bitcast.125) | data formatting | bytes 12582912
  96.9 8.7 %copy.35 = bf16[1024,3072]{1,0:T(8,128)(2,1)} copy(bf16[1024,3072]{0,1:T(8,128)(2,1)} %bitcast.120) | data formatting | bytes 12582912 | tf_op jit(solution)/shard_map/dot_general | solution.py:113
  107.4 2.0 fusion.32
  109.4 4.0 %fusion.51 = f32[256,2,4,128]{3,0,2,1:T(8,128)S(1)} fusion(bf16[2,4,128,3072]{3,2,1,0:T(8,128)(2,1)} %bitcast.126, bf16[256,3072]{1,0:T(8,128)(2,1)S(1)} %copy-done.2, f32[3072]{0:T(1024)S(1)} %bitcast.140, f32[3072]{0:T(1024)S(1)} %bitcast.139, f32[256]{0:T(256)S(1)} %add_rsqrt_fusion.3, f32[256]{0:T(256)S(1)} %broadcast_multiply_fusion), kind=kOutput, calls=%fused_computation.59 | convolution fusion | flops 1615331328 | bytes 8939520 | tf_op jit(solution)/shard_map/dot_general | solution.py:113
  114.7 28.4 %collective-permute-done.2 = bf16[2,256,3072]{2,1,0:T(8,128)(2,1)} collective-permute-done((bf16[2,256,3072]{2,1,0:T(8,128)(2,1)}, bf16[2,256,3072]{2,1,0:T(8,128)(2,1)}, u32[]{:S(2)}, u32[]{:S(2)}) %collective-permute-start.2) | collective-permute-done | bytes 3145760 | tf_op jit(solution)/shard_map/ppermute | solution.py:22
  143.0 2.6 %pad_maximum_fusion = bf16[2,2,256,3072]{3,2,1,0:T(8,128)(2,1)S(1)} fusion(bf16[1,2,256,3072]{3,2,1,0:T(8,128)(2,1)} %bitcast.21, bf16[1,2,256,3072]{3,2,1,0:T(8,128)(2,1)S(1)} %get-tuple-element.47), kind=kLoop, calls=%fused_computation.20 | loop fusion | flops 3145728 | bytes 12582912 | tf_op jit(solution)/shard_map/stack | solution.py:23
  145.6 4.4 %reverse_select_fusion = bf16[2,2,256,3072]{3,2,1,0:T(8,128)(2,1)} fusion(bf16[2,2,256,3072]{3,2,1,0:T(8,128)(2,1)S(1)} %pad_maximum_fusion, pred[]{:T(512)S(6)} %eq.6), kind=kLoop, calls=%fused_computation.19 | loop fusion | flops 3145728 | bytes 12582913 | tf_op jit(solution)/shard_map/jit(_where)/select_n | solution.py:25
  150.0 12.3 %fusion.74 = f32[1024,3,4,128]{3,0,2,1:T(8,128)S(1)} fusion(bf16[1024,3072,1,1]{1,0,3,2:T(8,128)(2,1)} %bitcast.127, bf16[3,4,128,3072]{3,2,1,0:T(8,128)(2,1)S(1)} %bitcast.123), kind=kOutput, calls=%fused_computation.97 | convolution fusion | flops 9663676416 | bytes 22020096 | tf_op jit(solution)/shard_map/dot_general | solution.py:105
  166.2 29.8 %while.10 = (s32[]{:T(128)}, bf16[2,512,4,128]{3,2,1,0:T(4,128)(2,1)}, bf16[2,512,4,128]{3,1,2,0:T(8,128)(2,1)}, bf16[1280,4,128]{2,0,1:T(8,128)(2,1)S(1)}, bf16[1280,4,128]{2,0,1:T(8,128)(2,1)S(1)}, /*index=5*/s32[]{:T(128)}) while((s32[]{:T(128)}, bf16[2,512,4,128]{3,2,1,0:T(4,128)(2,1)}, bf16[2,512,4,128]{3,1,2,0:T(8,128)(2,1)}, ...), condition=%wide.region_10.11_spmd, body=%wide.region_7.10_spmd.sunk | while | flops 1355547904 | bytes 25707588 | solution.py:123
  166.2 8.1 %fusion.94 = (f32[4,512]{1,0:T(4,128)S(1)}, f32[4,512,1280]{2,1,0:T(8,128)}) fusion(bf16[1280,4,128]{2,0,1:T(8,128)(2,1)S(1)} %get-tuple-element.109, bf16[2,512,4,128]{3,1,2,0:T(8,128)(2,1)} %get-tuple-element.108, s32[]{:T(128)} %get-tuple-element.100), kind=kOutput, calls=%fused_computation.95.clone.1 | convolution fusion | flops 678954240 | bytes 12329472 | tf_op jit(solution)/shard_map/while/body/eval_jaxpr/sub | solution.py:58
  174.4 5.5 %fusion.95 = bf16[1,512,4,128]{3,1,2,0:T(8,128)(2,1)S(1)} fusion(bf16[1280,4,128]{2,0,1:T(8,128)(2,1)S(1)} %get-tuple-element.110, f32[4,512,1280]{2,1,0:T(8,128)} %get-tuple-element.92, f32[4,512]{1,0:T(4,128)S(1)} %get-tuple-element.93), kind=kOutput, calls=%fused_computation.8.clone.1 | convolution fusion | flops 676593664 | bytes 12328960 | tf_op jit(solution)/shard_map/while/body/eval_jaxpr/hbk,khd->bhd/dot_general | solution.py:60
  181.1 8.1 %fusion.94 = (f32[4,512]{1,0:T(4,128)S(1)}, f32[4,512,1280]{2,1,0:T(8,128)}) fusion(bf16[1280,4,128]{2,0,1:T(8,128)(2,1)S(1)} %get-tuple-element.109, bf16[2,512,4,128]{3,1,2,0:T(8,128)(2,1)} %get-tuple-element.108, s32[]{:T(128)} %get-tuple-element.100), kind=kOutput, calls=%fused_computation.95.clone.1 | convolution fusion | flops 678954240 | bytes 12329472 | tf_op jit(solution)/shard_map/while/body/eval_jaxpr/sub | solution.py:58
  189.3 5.5 %fusion.95 = bf16[1,512,4,128]{3,1,2,0:T(8,128)(2,1)S(1)} fusion(bf16[1280,4,128]{2,0,1:T(8,128)(2,1)S(1)} %get-tuple-element.110, f32[4,512,1280]{2,1,0:T(8,128)} %get-tuple-element.92, f32[4,512]{1,0:T(4,128)S(1)} %get-tuple-element.93), kind=kOutput, calls=%fused_computation.8.clone.1 | convolution fusion | flops 676593664 | bytes 12328960 | tf_op jit(solution)/shard_map/while/body/eval_jaxpr/hbk,khd->bhd/dot_general | solution.py:60
  197.6 13.6 %all_to_all.34 = bf16[4,256,512]{2,1,0:T(8,128)(2,1)} all-to-all(bf16[4,256,512]{2,1,0:T(8,128)(2,1)S(1)} %all_to_all.28), channel_id=1, replica_groups=mesh['dp'=8,'ctx'=4] {'ctx'}, dimensions={0} | all-to-all | bytes 2097152 | tf_op jit(solution)/shard_map/all_to_all | solution.py:125
  (81 shorter events, 28.7 us)
Async XLA Ops:
  0.0 19.3 %copy-start = (bf16[3,3,3,128,256]{4,3,2,1,0:T(8,128)(2,1)S(1)}, bf16[3,3,3,128,256]{4,3,2,1,0:T(8,128)(2,1)}, u32[]{:S(2)}) copy-start(bf16[3,3,3,128,256]{4,3,2,1,0:T(8,128)(2,1)} %param.12) | copy-start | bytes 5308420
  1.1 7.6 %collective-permute-start = (bf16[8,1,64,128]{3,2,1,0:T(8,128)(2,1)S(1)}, bf16[8,1,64,128]{3,2,1,0:T(8,128)(2,1)S(1)}, u32[]{:S(2)}, u32[]{:S(2)}) collective-permute-start(bf16[8,1,64,128]{3,2,1,0:T(8,128)(2,1)S(1)} %slice.43), channel_id=1, source_target_pairs={{0,1},{1,2},{2,3},{4,5},{5,6},{6,7},{8,9},{9,10},{10,11},{12,13},{... | collective-permute-start | bytes 393224 | tf_op jit(solution)/shard_map/ppermute | solution.py:36
  16.8 2.6 %copy-start.12 = (pred[8,5]{0,1:T(8,128)(4,1)S(1)}, pred[8,5]{0,1:T(8,128)(4,1)}, u32[]{:S(2)}) copy-start(pred[8,5]{0,1:T(8,128)(4,1)} %constant.56) | copy-start | bytes 124
  22.0 1.1 copy-start.11
  22.0 7.7 %copy-start.7 = (f32[4,3072]{1,0:T(4,128)S(1)}, f32[4,3072]{1,0:T(4,128)}, u32[]{:S(2)}) copy-start(f32[4,3072]{1,0:T(4,128)} %param.15) | copy-start | bytes 147460
  22.0 12.5 %copy-start.4 = (bf16[64,3072]{1,0:T(8,128)(2,1)S(1)}, bf16[64,3072]{1,0:T(8,128)(2,1)}, u32[]{:S(2)}) copy-start(bf16[64,3072]{1,0:T(8,128)(2,1)} %param.14) | copy-start | bytes 1179652
  24.9 9.5 %all-to-all-start = ((bf16[4,2,2048]{2,1,0:T(2,128)(2,1)}), bf16[4,2,2048]{2,1,0:T(2,128)(2,1)S(1)}, u32[]{:S(2)}, u32[]{:S(2)}) async-start(bf16[4,2,2048]{2,1,0:T(2,128)(2,1)} %reshape.116), calls=%async_computation | async-start | bytes 65536 | tf_op jit(solution)/shard_map/all_to_all | solution.py:94
  34.6 1.1 copy-start.5
  35.7 2.6 %copy-start.6 = (f32[1,3072]{1,0:T(1,128)S(1)}, f32[1,3072]{1,0:T(1,128)}, u32[]{:S(2)}) copy-start(f32[1,3072]{1,0:T(1,128)} %get-tuple-element.51) | copy-start | bytes 36868
  37.5 34.1 %collective-permute-start.1 = (bf16[1,256,3072]{2,1,0:T(8,128)(2,1)}, bf16[1,256,3072]{2,1,0:T(8,128)(2,1)}, u32[]{:S(2)}, u32[]{:S(2)}) collective-permute-start(bf16[1,256,3072]{2,1,0:T(8,128)(2,1)} %fusion.85), channel_id=1, source_target_pairs={{0,1},{1,0},{2,3},{3,2},{4,5},{5,4},{6,7},{7,6},{8,9},{9,8},{10,11... | collective-permute-start | bytes 4718600 | tf_op jit(solution)/shard_map/ppermute | solution.py:22
  76.1 66.9 %collective-permute-start.2 = (bf16[2,256,3072]{2,1,0:T(8,128)(2,1)}, bf16[2,256,3072]{2,1,0:T(8,128)(2,1)}, u32[]{:S(2)}, u32[]{:S(2)}) collective-permute-start(bf16[2,256,3072]{2,1,0:T(8,128)(2,1)} %get-tuple-element.48), channel_id=1, source_target_pairs={{0,2},{1,3},{2,0},{3,1},{4,6},{5,7},{6,4},{7,5},{8,10},{9,11},{10,... | collective-permute-start | bytes 9437192 | tf_op jit(solution)/shard_map/ppermute | solution.py:22
  105.6 3.8 %copy-start.2 = (bf16[256,3072]{1,0:T(8,128)(2,1)S(1)}, bf16[256,3072]{1,0:T(8,128)(2,1)}, u32[]{:S(2)}) copy-start(bf16[256,3072]{1,0:T(8,128)(2,1)} %param.18) | copy-start | bytes 4718596
  105.6 3.8 %copy-start.8 = (f32[1,3072]{1,0:T(1,128)S(1)}, f32[1,3072]{1,0:T(1,128)}, u32[]{:S(2)}) copy-start(f32[1,3072]{1,0:T(1,128)} %get-tuple-element.49) | copy-start | bytes 36868
  105.6 3.8 %copy-start.9 = (f32[1,3072]{1,0:T(1,128)S(1)}, f32[1,3072]{1,0:T(1,128)}, u32[]{:S(2)}) copy-start(f32[1,3072]{1,0:T(1,128)} %get-tuple-element.52) | copy-start | bytes 36868
  109.4 4.3 %copy-start.10 = (f32[2,128]{1,0:T(2,128)S(1)}, f32[2,128]{1,0:T(2,128)}, u32[]{:S(2)}) copy-start(f32[2,128]{1,0:T(2,128)} %param.17) | copy-start | bytes 3076
  143.0 7.0 %slice-start = ((s8[9437184]{0:T(1024)(128)(4,1)}), s8[4194304]{0:T(1024)(128)(4,1)S(1)}, s32[]{:S(2)}) async-start(s8[9437184]{0:T(1024)(128)(4,1)} %bitcast.121), calls=%async_computation.2 | async-start | bytes 8388608
  143.0 7.0 %slice-start.1 = ((s8[9437184]{0:T(1024)(128)(4,1)}), s8[4194304]{0:T(1024)(128)(4,1)S(1)}, s32[]{:S(2)}) async-start(s8[9437184]{0:T(1024)(128)(4,1)} %bitcast.121), calls=%async_computation.3 | async-start | bytes 8388608
  145.6 4.4 %slice-start.2 = ((s8[9437184]{0:T(1024)(128)(4,1)}), s8[1048576]{0:T(1024)(128)(4,1)S(1)}, s32[]{:S(2)}) async-start(s8[9437184]{0:T(1024)(128)(4,1)} %bitcast.121), calls=%async_computation.4 | async-start | bytes 2097152
  163.8 2.3 %copy-start.3 = (bf16[256,4,128]{2,0,1:T(8,128)(2,1)S(1)}, bf16[256,4,128]{2,0,1:T(8,128)(2,1)}, u32[]{:S(2)}) copy-start(bf16[256,4,128]{2,0,1:T(8,128)(2,1)} %multiply_convert_fusion.2) | copy-start | bytes 786436
  196.0 18.1 %copy-start.1 = (bf16[3,3,3,128,256]{4,3,2,1,0:T(8,128)(2,1)S(1)}, bf16[3,3,3,128,256]{4,3,2,1,0:T(8,128)(2,1)}, u32[]{:S(2)}) copy-start(bf16[3,3,3,128,256]{4,3,2,1,0:T(8,128)(2,1)} %param.12) | copy-start | bytes 5308420
